TPU v7x, 256 devices: a whole 4x4x8 slice. The times are simulated.
256 devices in a mesh: dp: 4 (over x), seq: 16 (over z, core), tensor: 4 (over y).
Axes of the slice: x: 4, y: 4, z: 8, core: 2. Of those that a mesh axis runs over, the one named last changes fastest.
Arguments:
- feature_in: bfloat16 [16, 2048, 512], P('dp', 'seq', 'tensor'), may hold values from -6 to 6
- conv_weight: bfloat16 [2, 512, 512], P(None, 'tensor'), may hold values from -0.1875 to 0.1875
- proj_weight: bfloat16 [512, 1920], P(None, 'tensor'), may hold values from -0.25 to 0.25
- mask_embed: bfloat16 [1920], P('tensor'), may hold values from -5 to 5
- pos_weight: bfloat16 [128, 16, 120, 120], P(('dp', 'seq'), 'tensor'), may hold values from -0.046875 to 0.046875
- final_weight: bfloat16 [1920, 1024], P('tensor'), may hold values from -0.125 to 0.125
- codebook: bfloat16 [2, 320, 512], replicated, may hold values from -6 to 6
- quant_weight: bfloat16 [1024, 1024], replicated, may hold values from -0.1875 to 0.1875
- mask_starts: int32 [16, 66], P('dp'), may hold values from 0 to 1014
- code_choice: int32 [16, 1024, 2], P(('dp', 'tensor'), 'seq'), may hold values from 0 to 319
- negative_ids: int32 [16, 1024, 100], P(('dp', 'tensor'), 'seq'), may hold values from 0 to 1023, as said below
Outputs:
- frame_loss: float32 [16, 1024], P(('dp', 'tensor'), 'seq')
Inputs may be any that keep to these rules, and one draw needn't show every extreme that they name: `negative_ids`: each entry names a frame of the same utterance other than the frame itself.
All inputs are finite; a program needn't handle non-finite values.
Results may differ from a plain program's by a relative error of at most 0.00065.
Values may be sent and summed in bfloat16 or wider, within the bound.
A program may use at most 128 MiB of HBM per device.

v0:
```python
import jax
import jax.numpy as jnp
from jax import lax
from jax.sharding import PartitionSpec as P

KERNEL = 128
MASK_LEN = 10
ln_eps = 1e-05
norm_eps = 1e-06
logit_temp = 0.1


def extended(block, sides, width):
    for axis, dim in sides:
        count = lax.axis_size(axis)
        forward = [(i, i + 1) for i in range(count - 1)]
        backward = [(target, source) for source, target in forward]
        low = lax.ppermute(
            lax.slice_in_dim(block, block.shape[dim] - width, None, axis=dim), axis, forward
        )
        high = lax.ppermute(lax.slice_in_dim(block, 0, width, axis=dim), axis, backward)
        block = jnp.concatenate([low, block, high], axis=dim)
    return block


def make_targets(code_block, codebook, quant_weight):
    entries = codebook.shape[1]
    choices_row = jnp.arange(entries, dtype=jnp.int32)
    pieces = []
    for qgroup in range(codebook.shape[0]):
        onehot = (code_block[..., qgroup, None] == choices_row).astype(jnp.bfloat16)
        pieces.append(
            jnp.dot(onehot, codebook[qgroup], preferred_element_type=jnp.float32).astype(
                jnp.bfloat16
            )
        )
    codevec = jnp.concatenate(pieces, axis=-1)
    return jnp.dot(codevec, quant_weight, preferred_element_type=jnp.float32).astype(jnp.bfloat16)


def utterance_loss(context, own_targets, all_targets, neg_ids, is_masked):
    scores = jnp.einsum("fc,nc->fn", context, all_targets, preferred_element_type=jnp.float32)
    ctx_norm = jnp.einsum("fc,fc->f", context, context, preferred_element_type=jnp.float32)
    own_norm = jnp.einsum("fc,fc->f", own_targets, own_targets, preferred_element_type=jnp.float32)
    tgt_norm = jnp.einsum("nc,nc->n", all_targets, all_targets, preferred_element_type=jnp.float32)
    pos_dot = jnp.einsum("fc,fc->f", context, own_targets, preferred_element_type=jnp.float32)
    neg_dot = jnp.take_along_axis(scores, neg_ids, axis=1)
    neg_norm = tgt_norm[neg_ids]
    positive = pos_dot * lax.rsqrt((ctx_norm + norm_eps) * (own_norm + norm_eps)) / logit_temp
    negative = (
        neg_dot * lax.rsqrt((ctx_norm[:, None] + norm_eps) * (neg_norm + norm_eps)) / logit_temp
    )
    frame_loss = jnp.log(jnp.exp(positive) + jnp.sum(jnp.exp(negative), axis=-1)) - positive
    return jnp.where(is_masked, frame_loss, jnp.zeros_like(frame_loss))


def tap_sum(windows, running, tap_block, frames):
    count = tap_block.shape[0]
    joined_taps = max((d for d in range(1, 17) if count % d == 0))
    group_count, inner, outer = (tap_block.shape[1], tap_block.shape[2], tap_block.shape[3])

    def add_block(step, partial_value):
        base = step * joined_taps
        slabs = [
            lax.dynamic_slice_in_dim(windows, base + offset, frames, 1)
            for offset in range(joined_taps)
        ]
        joined = jnp.concatenate(slabs, axis=-1)
        taps = lax.dynamic_slice_in_dim(tap_block, base, joined_taps, 0)
        taps = jnp.transpose(taps, (1, 0, 2, 3)).reshape(group_count, joined_taps * inner, outer)
        return partial_value + jnp.einsum(
            "ufgi,gio->ufgo", joined, taps, preferred_element_type=jnp.float32
        )

    return lax.fori_loop(0, count // joined_taps, add_block, running)


def on_device(
    feature_in,
    conv_weight,
    proj_weight,
    mask_embed,
    pos_weight,
    final_weight,
    codebook,
    quant_weight,
    mask_starts,
    code_choice,
    negative_ids,
):
    utt_count, sample_rows, channels = feature_in.shape
    frames = sample_rows // 2
    frame_pairs = feature_in.reshape(utt_count, frames, 2 * channels)
    conv_term = jnp.dot(
        frame_pairs,
        conv_weight.reshape(2 * channels, conv_weight.shape[2]),
        preferred_element_type=jnp.float32,
    )
    summed = lax.psum(conv_term, "tensor")
    row_mean = jnp.mean(summed, axis=-1, keepdims=True)
    row_square = jnp.mean(summed * summed, axis=-1, keepdims=True)
    normed = (summed - row_mean) * lax.rsqrt(row_square - row_mean * row_mean + ln_eps)
    features = jax.nn.gelu(normed, approximate=False).astype(jnp.bfloat16)
    projected = jnp.dot(features, proj_weight, preferred_element_type=jnp.float32).astype(
        jnp.bfloat16
    )
    positions = (lax.axis_index("seq") * frames + jnp.arange(frames, dtype=jnp.int32))[
        None, :, None
    ]
    starts = mask_starts[:, None, :]
    masked = jnp.any((positions >= starts) & (positions < starts + MASK_LEN), axis=-1)
    hidden = jnp.where(masked[..., None], mask_embed[None, None, :], projected)
    padded = extended(hidden, (("seq", 1),), KERNEL // 2)
    group_count = pos_weight.shape[1]
    inner = pos_weight.shape[2]
    outer = pos_weight.shape[3]
    windows = padded.reshape(utt_count, padded.shape[1], group_count, inner)
    initial = jnp.zeros((utt_count, frames, group_count, outer), jnp.float32)
    conv_out = tap_sum(
        windows, initial, lax.all_gather(pos_weight, ("dp", "seq"), axis=0, tiled=True), frames
    )
    conv_out = conv_out.reshape(utt_count, frames, group_count * outer)
    mixed = (hidden.astype(jnp.float32) + jax.nn.gelu(conv_out, approximate=False)).astype(
        jnp.bfloat16
    )
    utt_rows = utt_count // lax.axis_size("tensor")
    context = lax.psum_scatter(
        jnp.dot(mixed, final_weight, preferred_element_type=jnp.float32),
        "tensor",
        scatter_dimension=0,
        tiled=True,
    ).astype(jnp.bfloat16)
    own_targets = make_targets(code_choice, codebook, quant_weight)
    all_targets = lax.all_gather(own_targets, "seq", axis=1, tiled=True)
    is_masked = lax.dynamic_slice_in_dim(masked, lax.axis_index("tensor") * utt_rows, utt_rows, 0)
    return jax.vmap(utterance_loss)(context, own_targets, all_targets, negative_ids, is_masked)


def solution(mesh):
    return jax.shard_map(
        on_device,
        mesh=mesh,
        in_specs=(
            P("dp", "seq", "tensor"),
            P(None, "tensor", None),
            P(None, "tensor"),
            P("tensor"),
            P(("dp", "seq"), "tensor", None, None),
            P("tensor", None),
            P(),
            P(),
            P("dp", None),
            P(("dp", "tensor"), "seq", None),
            P(("dp", "tensor"), "seq", None),
        ),
        out_specs=P(("dp", "tensor"), "seq"),
        check_vma=False,
    )
```

profile of v0, /device:TPU:1, one launch (start us, length us, event | category | flops | bytes accessed | tf_op | source)
XLA Modules:
  0.0 506.4 jit_solution(2708013920155017598)
XLA Ops:
  8.5 2.0 fusion.176
  12.7 48.5 %all-reduce.2.cloned.1.call-done = f32[4,64,512]{2,1,0:T(8,128)} async-done(((f32[4,64,512]{2,1,0:T(8,128)}), f32[4,64,512]{2,1,0:T(8,128)}) %all-reduce.2.cloned.1.call-update) | async-done | bytes 524304 | tf_op jit(solution)/shard_map/psum | solution.py:99
  62.4 2.6 fusion.1
  65.0 5.1 %collective-permute-start = (bf16[4,64,480]{2,1,0:T(8,128)(2,1)S(1)}, bf16[4,64,480]{2,1,0:T(8,128)(2,1)S(1)}, u32[]{:S(2)}, u32[]{:S(2)}) collective-permute-start(bf16[4,64,480]{2,1,0:T(8,128)(2,1)S(1)} %fusion.1), channel_id=1, source_target_pairs={{0,4},{4,8},{8,12},{12,16},{16,20},{20,24},{24,28},{28,32},{32,36}... | collective-permute-start | bytes 737288 | tf_op jit(solution)/shard_map/ppermute | solution.py:18
  72.0 6.7 %collective-permute-done = bf16[4,64,480]{2,1,0:T(8,128)(2,1)S(1)} collective-permute-done((bf16[4,64,480]{2,1,0:T(8,128)(2,1)S(1)}, bf16[4,64,480]{2,1,0:T(8,128)(2,1)S(1)}, u32[]{:S(2)}, u32[]{:S(2)}) %collective-permute-start) | collective-permute-done | bytes 245792 | tf_op jit(solution)/shard_map/ppermute | solution.py:18
  78.8 4.0 collective-permute-done.1
  86.5 28.4 %all-gather.4.cloned.1.call-done = bf16[128,4,120,120]{3,2,1,0:T(8,128)(2,1)} async-done(((bf16[2,4,120,120]{3,2,1,0:T(8,128)(2,1)}), bf16[128,4,120,120]{3,2,1,0:T(8,128)(2,1)}) %all-gather.4.cloned.1.call-update) | async-done | bytes 14745616 | tf_op jit(solution)/shard_map/all_gather | solution.py:120
  114.9 222.5 %while.16 = (s32[]{:T(128)}, f32[4,64,4,120]{3,1,0,2:T(8,128)}, bf16[128,4,120,120]{3,2,1,0:T(8,128)(2,1)}, bf16[4,192,4,120]{3,1,0,2:T(8,128)(2,1)S(1)}, s32[]{...) while((s32[]{:T(128)}, f32[4,64,4,120]{3,1,0,2:T(8,128)}, ...), condition=%wide.region_5.6_spmd.clone, body=%wide.region_4.5_spmd.clone.sunk | while | flops 472105024 | bytes 34530440 | solution.py:75
  114.9 2.9 constant_dynamic-slice_fusion.20
  117.9 7.1 %concatenate.26 = bf16[4,64,4,1920]{3,1,0,2:T(8,128)(2,1)} concatenate(bf16[4,64,4,120]{3,1,0,2:T(8,128)(2,1)} %get-tuple-element.238, bf16[4,64,4,120]{3,1,0,2:T(8,128)(2,1)} %get-tuple-element.239, bf16[4,64,4,120]{3,1,0,2:T(8,128)(2,1)} %get-tuple-element.240, bf16[4,64,4,120]{3,1,0,2:T(8,128)(2,1)} %get-tuple-element.241, bf16[4,64,4,120]{3,1,0,2:T(8,128)(2,1)} %get-tuple-element.242, ...), dimensions={3} | concatenate | bytes 7864320 | tf_op jit(solution)/shard_map/while/body/eval_jaxpr/concatenate | solution.py:68
  125.0 3.0 constant_dynamic-slice_fusion.19
  128.0 4.4 copy.47
  132.5 4.6 reshape.312
  137.1 3.8 fusion.188
  141.8 3.0 constant_dynamic-slice_fusion.20
  144.8 7.1 %concatenate.26 = bf16[4,64,4,1920]{3,1,0,2:T(8,128)(2,1)} concatenate(bf16[4,64,4,120]{3,1,0,2:T(8,128)(2,1)} %get-tuple-element.238, bf16[4,64,4,120]{3,1,0,2:T(8,128)(2,1)} %get-tuple-element.239, bf16[4,64,4,120]{3,1,0,2:T(8,128)(2,1)} %get-tuple-element.240, bf16[4,64,4,120]{3,1,0,2:T(8,128)(2,1)} %get-tuple-element.241, bf16[4,64,4,120]{3,1,0,2:T(8,128)(2,1)} %get-tuple-element.242, ...), dimensions={3} | concatenate | bytes 7864320 | tf_op jit(solution)/shard_map/while/body/eval_jaxpr/concatenate | solution.py:68
  151.9 3.0 constant_dynamic-slice_fusion.19
  154.9 4.4 copy.47
  159.4 4.6 reshape.312
  164.0 3.8 fusion.188
  169.7 3.0 constant_dynamic-slice_fusion.20
  172.7 7.1 %concatenate.26 = bf16[4,64,4,1920]{3,1,0,2:T(8,128)(2,1)} concatenate(bf16[4,64,4,120]{3,1,0,2:T(8,128)(2,1)} %get-tuple-element.238, bf16[4,64,4,120]{3,1,0,2:T(8,128)(2,1)} %get-tuple-element.239, bf16[4,64,4,120]{3,1,0,2:T(8,128)(2,1)} %get-tuple-element.240, bf16[4,64,4,120]{3,1,0,2:T(8,128)(2,1)} %get-tuple-element.241, bf16[4,64,4,120]{3,1,0,2:T(8,128)(2,1)} %get-tuple-element.242, ...), dimensions={3} | concatenate | bytes 7864320 | tf_op jit(solution)/shard_map/while/body/eval_jaxpr/concatenate | solution.py:68
  179.9 3.0 constant_dynamic-slice_fusion.19
  182.9 4.4 copy.47
  187.3 4.6 reshape.312
  191.9 3.8 fusion.188
  197.7 3.0 constant_dynamic-slice_fusion.20
  200.7 7.1 %concatenate.26 = bf16[4,64,4,1920]{3,1,0,2:T(8,128)(2,1)} concatenate(bf16[4,64,4,120]{3,1,0,2:T(8,128)(2,1)} %get-tuple-element.238, bf16[4,64,4,120]{3,1,0,2:T(8,128)(2,1)} %get-tuple-element.239, bf16[4,64,4,120]{3,1,0,2:T(8,128)(2,1)} %get-tuple-element.240, bf16[4,64,4,120]{3,1,0,2:T(8,128)(2,1)} %get-tuple-element.241, bf16[4,64,4,120]{3,1,0,2:T(8,128)(2,1)} %get-tuple-element.242, ...), dimensions={3} | concatenate | bytes 7864320 | tf_op jit(solution)/shard_map/while/body/eval_jaxpr/concatenate | solution.py:68
  207.8 3.0 constant_dynamic-slice_fusion.19
  210.9 4.4 copy.47
  215.3 4.6 reshape.312
  219.9 3.8 fusion.188
  225.6 2.9 constant_dynamic-slice_fusion.20
  228.6 7.1 %concatenate.26 = bf16[4,64,4,1920]{3,1,0,2:T(8,128)(2,1)} concatenate(bf16[4,64,4,120]{3,1,0,2:T(8,128)(2,1)} %get-tuple-element.238, bf16[4,64,4,120]{3,1,0,2:T(8,128)(2,1)} %get-tuple-element.239, bf16[4,64,4,120]{3,1,0,2:T(8,128)(2,1)} %get-tuple-element.240, bf16[4,64,4,120]{3,1,0,2:T(8,128)(2,1)} %get-tuple-element.241, bf16[4,64,4,120]{3,1,0,2:T(8,128)(2,1)} %get-tuple-element.242, ...), dimensions={3} | concatenate | bytes 7864320 | tf_op jit(solution)/shard_map/while/body/eval_jaxpr/concatenate | solution.py:68
  235.7 3.0 constant_dynamic-slice_fusion.19
  238.8 4.4 copy.47
  243.2 4.6 reshape.312
  247.8 3.8 fusion.188
  253.6 3.0 constant_dynamic-slice_fusion.20
  256.5 7.1 %concatenate.26 = bf16[4,64,4,1920]{3,1,0,2:T(8,128)(2,1)} concatenate(bf16[4,64,4,120]{3,1,0,2:T(8,128)(2,1)} %get-tuple-element.238, bf16[4,64,4,120]{3,1,0,2:T(8,128)(2,1)} %get-tuple-element.239, bf16[4,64,4,120]{3,1,0,2:T(8,128)(2,1)} %get-tuple-element.240, bf16[4,64,4,120]{3,1,0,2:T(8,128)(2,1)} %get-tuple-element.241, bf16[4,64,4,120]{3,1,0,2:T(8,128)(2,1)} %get-tuple-element.242, ...), dimensions={3} | concatenate | bytes 7864320 | tf_op jit(solution)/shard_map/while/body/eval_jaxpr/concatenate | solution.py:68
  263.7 3.0 constant_dynamic-slice_fusion.19
  266.7 4.4 copy.47
  271.2 4.6 reshape.312
  275.7 3.8 fusion.188
  281.5 3.0 constant_dynamic-slice_fusion.20
  284.5 7.1 %concatenate.26 = bf16[4,64,4,1920]{3,1,0,2:T(8,128)(2,1)} concatenate(bf16[4,64,4,120]{3,1,0,2:T(8,128)(2,1)} %get-tuple-element.238, bf16[4,64,4,120]{3,1,0,2:T(8,128)(2,1)} %get-tuple-element.239, bf16[4,64,4,120]{3,1,0,2:T(8,128)(2,1)} %get-tuple-element.240, bf16[4,64,4,120]{3,1,0,2:T(8,128)(2,1)} %get-tuple-element.241, bf16[4,64,4,120]{3,1,0,2:T(8,128)(2,1)} %get-tuple-element.242, ...), dimensions={3} | concatenate | bytes 7864320 | tf_op jit(solution)/shard_map/while/body/eval_jaxpr/concatenate | solution.py:68
  291.6 3.0 constant_dynamic-slice_fusion.19
  294.7 4.4 copy.47
  299.1 4.6 reshape.312
  303.7 3.9 fusion.188
  309.5 3.0 constant_dynamic-slice_fusion.20
  312.5 7.1 %concatenate.26 = bf16[4,64,4,1920]{3,1,0,2:T(8,128)(2,1)} concatenate(bf16[4,64,4,120]{3,1,0,2:T(8,128)(2,1)} %get-tuple-element.238, bf16[4,64,4,120]{3,1,0,2:T(8,128)(2,1)} %get-tuple-element.239, bf16[4,64,4,120]{3,1,0,2:T(8,128)(2,1)} %get-tuple-element.240, bf16[4,64,4,120]{3,1,0,2:T(8,128)(2,1)} %get-tuple-element.241, bf16[4,64,4,120]{3,1,0,2:T(8,128)(2,1)} %get-tuple-element.242, ...), dimensions={3} | concatenate | bytes 7864320 | tf_op jit(solution)/shard_map/while/body/eval_jaxpr/concatenate | solution.py:68
  319.6 3.0 constant_dynamic-slice_fusion.19
  322.7 4.4 copy.47
  327.1 4.6 reshape.312
  331.7 3.8 fusion.188
  340.7 3.8 fusion.4
  347.1 19.4 %reduce-scatter.2.cloned.1.call-done = f32[1,64,1024]{2,1,0:T(8,128)} async-done(((f32[4,64,1024]{2,1,0:T(8,128)}), f32[1,64,1024]{2,1,0:T(8,128)}) %reduce-scatter.2.cloned.1.call-update) | async-done | bytes 262160 | tf_op jit(solution)/shard_map/reduce_scatter | solution.py:127
  366.5 2.3 fusion.34
  369.3 41.1 %all-gather.6.cloned.1.call-done = bf16[1024,1024]{1,0:T(8,128)(2,1)} async-done(((bf16[64,1024]{1,0:T(8,128)(2,1)}), bf16[1024,1024]{1,0:T(8,128)(2,1)}) %all-gather.6.cloned.1.call-update) | async-done | bytes 2097168 | tf_op jit(solution)/shard_map/all_gather | solution.py:134
  410.3 2.3 convolution_bitcast_fusion
  412.7 48.5 %gather_fusion = f32[6400]{0:T(1024)S(1)} fusion(f32[1,64,1024]{2,1,0:T(8,128)S(1)} %convolution_bitcast_fusion, s32[6400]{0:T(1024)S(1)} %reshape.273), kind=kCustom, calls=%fused_computation | custom fusion | bytes 128000 | tf_op jit(solution)/shard_map/vmap(jit(take_along_axis))/gather | solution.py:47
  461.3 2.1 fusion
  463.3 35.1 %gather_fusion.1 = f32[6400]{0:T(1024)S(1)} fusion(f32[1,1024]{1,0:T(1,128)S(1)} %bitcast.82, s32[6400]{0:T(1024)S(1)} %reshape.281), kind=kCustom, calls=%fused_computation.1 | custom fusion | bytes 102400 | tf_op jit(solution)/shard_map/vmap()/gather | solution.py:48
  (62 shorter events, 31.7 us)
Async XLA Ops:
  7.4 359.2 %copy-start = (bf16[1024,1024]{1,0:T(8,128)(2,1)S(1)}, bf16[1024,1024]{1,0:T(8,128)(2,1)}, u32[]{:S(2)}) copy-start(bf16[1024,1024]{1,0:T(8,128)(2,1)} %param.20) | copy-start | bytes 6291460
  7.4 53.8 %all-reduce.2.cloned.1.call-start = ((), (), s32[]{:S(2)}) async-start(), calls=%async_computation.1 | async-start | bytes 1048576 | tf_op jit(solution)/shard_map/psum | solution.py:99
  10.5 104.4 %all-gather.4.cloned.1.call-start = ((), (), s32[]{:S(2)}) async-start(), calls=%async_computation.2 | async-start | bytes 15974400 | tf_op jit(solution)/shard_map/all_gather | solution.py:120
  11.1 355.5 %reduce-scatter.2.cloned.1.call-start = ((), (), s32[]{:S(2)}) async-start(), calls=%async_computation.3 | async-start | bytes 1310720 | tf_op jit(solution)/shard_map/reduce_scatter | solution.py:127
  65.0 49.9 %copy-start.2 = (bf16[4,64,480]{2,1,0:T(8,128)(2,1)}, bf16[4,64,480]{2,1,0:T(8,128)(2,1)S(1)}, u32[]{:S(2)}) copy-start(bf16[4,64,480]{2,1,0:T(8,128)(2,1)S(1)} %fusion.1) | copy-start | bytes 737284
  65.0 13.7 %collective-permute-start = (bf16[4,64,480]{2,1,0:T(8,128)(2,1)S(1)}, bf16[4,64,480]{2,1,0:T(8,128)(2,1)S(1)}, u32[]{:S(2)}, u32[]{:S(2)}) collective-permute-start(bf16[4,64,480]{2,1,0:T(8,128)(2,1)S(1)} %fusion.1), channel_id=1, source_target_pairs={{0,4},{4,8},{8,12},{12,16},{16,20},{20,24},{24,28},{28,32},{32,36}... | collective-permute-start | bytes 737288 | tf_op jit(solution)/shard_map/ppermute | solution.py:18
  70.1 12.7 %collective-permute-start.1 = (bf16[4,64,480]{2,1,0:T(8,128)(2,1)S(1)}, bf16[4,64,480]{2,1,0:T(8,128)(2,1)}, u32[]{:S(2)}, u32[]{:S(2)}) collective-permute-start(bf16[4,64,480]{2,1,0:T(8,128)(2,1)S(1)} %fusion.1), channel_id=1, source_target_pairs={{4,0},{8,4},{12,8},{16,12},{20,16},{24,20},{28,24},{32,28},{36,32}... | collective-permute-start | bytes 737288 | tf_op jit(solution)/shard_map/ppermute | solution.py:21
  337.5 3.2 copy-start.3
  340.7 4.1 copy-start.5
  344.5 24.4 %copy-start.4 = (s32[1,64,100]{2,1,0:T(8,128)S(1)}, s32[1,64,100]{2,1,0:T(8,128)}, u32[]{:S(2)}) copy-start(s32[1,64,100]{2,1,0:T(8,128)} %param.23) | copy-start | bytes 76804
  344.5 65.8 %all-gather.6.cloned.1.call-start = ((), (), s32[]{:S(2)}) async-start(), calls=%async_computation.4 | async-start | bytes 2228224 | tf_op jit(solution)/shard_map/all_gather | solution.py:134
  366.5 43.8 %copy-start.1 = (f32[1,64,1024]{2,1,0:T(8,128)S(1)}, f32[1,64,1024]{2,1,0:T(8,128)}, u32[]{:S(2)}) copy-start(f32[1,64,1024]{2,1,0:T(8,128)} %reduce-scatter.2.cloned.1.call-done) | copy-start | bytes 786436
Sparse Core Ops, SparseCore 0:
  10.6 50.5 all-reduce.1
  344.6 21.8 reduce-scatter.1
  369.0 41.2 all-gather.5
Sparse Core Ops, SparseCore 1:
  13.7 101.2 all-gather.3
where the time goes:
time: 514 us; the launch traced here: 506 us
  local copies, waits for them, and re-layouts  267 us (52%)
  waiting for transfers between devices  149 us (29%)
  matrix products  46.2 us (9%)
  other arithmetic  22.3 us (4%)
  between operations  14.8 us (3%)
  starting transfers between devices  7.3 us (1%)
    dynamic_slice x16, local copies, waits for them, and re-layouts, add_block(): taps = lax.dynamic_slice_in_dim(tap_block, base, joined_taps, 0)  59.7 us
    concatenate x8, local copies, waits for them, and re-layouts, add_block(): joined = jnp.concatenate(slabs, axis=-1)  57.2 us
    gather x4, local copies, waits for them, and re-layouts, utterance_loss(): neg_dot = jnp.take_along_axis(scores, neg_ids, axis=1)  48.7 us
    psum x1, waiting for transfers between devices, on_device(): summed = lax.psum(conv_term, 'tensor')  48.5 us
    all_gather x1, waiting for transfers between devices, on_device(): all_targets = lax.all_gather(own_targets, 'seq', axis=1, tiled=True)  41.1 us
    reshape x8, local copies, waits for them, and re-layouts, add_block(): jnp.transpose(taps, (1, 0, 2, 3))  36.6 us
    gather x3, local copies, waits for them, and re-layouts, utterance_loss(): neg_norm = tgt_norm[neg_ids]  35.2 us
    while x8, matrix products  30.8 us
  transfers between devices with their start and end apart: 6, of which 6 were waited for; matrix products, arithmetic and copies ran while one was open for 2% of the time, Pallas kernels for 0%

commit v1 on v0

--- a/solution.py
+++ b/solution.py
@@ -96,7 +96,7 @@
         conv_weight.reshape(2 * channels, conv_weight.shape[2]),
         preferred_element_type=jnp.float32,
     )
-    summed = lax.psum(conv_term, "tensor")
+    summed = jnp.sum(lax.all_gather(conv_term, "tensor"), axis=0)
     row_mean = jnp.mean(summed, axis=-1, keepdims=True)
     row_square = jnp.mean(summed * summed, axis=-1, keepdims=True)
     normed = (summed - row_mean) * lax.rsqrt(row_square - row_mean * row_mean + ln_eps)

time: 514 us -> 545 us (1.060)
  waiting for transfers between devices: 149 us -> 180 us
    all_gather x1, waiting for transfers between devices: 28.4 us -> 78.8 us  [on_device(): lax.all_gather(pos_weight, ('dp', 'seq'), axis=0, tiled=True)]
    psum x1 -> x0, waiting for transfers between devices: 48.5 us -> none  [on_device(): summed = lax.psum(conv_term, 'tensor')]
    all_gather x0 -> x1, waiting for transfers between devices: none -> 35 us  [on_device(): summed = jnp.sum(lax.all_gather(conv_term, 'tensor'), axis=0)]
  transfers between devices with their start and end apart: 6 -> 6, of which waited for: 6 -> 6; matrix products, arithmetic and copies ran while one was open for 2% -> 3% of each run, Pallas kernels for 0% -> 0%
where the time goes in v1:
time: 545 us; the launch traced here: 538 us
  local copies, waits for them, and re-layouts  267 us (49%)
  waiting for transfers between devices  180 us (33%)
  matrix products  46 us (8%)
  other arithmetic  24.9 us (5%)
  between operations  13.4 us (2%)
  starting transfers between devices  5.96 us (1%)
    all_gather x1, waiting for transfers between devices, on_device(): lax.all_gather(pos_weight, ('dp', 'seq'), axis=0, tiled=True)  78.8 us
    dynamic_slice x16, local copies, waits for them, and re-layouts, add_block(): taps = lax.dynamic_slice_in_dim(tap_block, base, joined_taps, 0)  59.7 us
    concatenate x8, local copies, waits for them, and re-layouts, add_block(): joined = jnp.concatenate(slabs, axis=-1)  57.2 us
    gather x4, local copies, waits for them, and re-layouts, utterance_loss(): neg_dot = jnp.take_along_axis(scores, neg_ids, axis=1)  48.7 us
    all_gather x1, waiting for transfers between devices, on_device(): all_targets = lax.all_gather(own_targets, 'seq', axis=1, tiled=True)  41 us
    reshape x8, local copies, waits for them, and re-layouts, add_block(): jnp.transpose(taps, (1, 0, 2, 3))  36.6 us
    gather x3, local copies, waits for them, and re-layouts, utterance_loss(): neg_norm = tgt_norm[neg_ids]  35.2 us
    all_gather x1, waiting for transfers between devices, on_device(): summed = jnp.sum(lax.all_gather(conv_term, 'tensor'), axis=0)  35 us
  transfers between devices with their start and end apart: 6, of which 6 were waited for; matrix products, arithmetic and copies ran while one was open for 3% of the time, Pallas kernels for 0%

profile of v1, /device:TPU:1, one launch (start us, length us, event | category | flops | bytes accessed | tf_op | source)
XLA Modules:
  0.0 537.7 jit_solution(7318156916189150504)
XLA Ops:
  7.7 2.0 fusion.175
  12.1 35.0 %all-gather.8.cloned.1.call-done = f32[16,64,512]{2,1,0:T(8,128)} async-done(((f32[4,64,512]{2,1,0:T(8,128)}), f32[16,64,512]{2,1,0:T(8,128)}) %all-gather.8.cloned.1.call-update) | async-done | bytes 2097168 | tf_op jit(solution)/shard_map/all_gather | solution.py:99
  50.9 2.4 fusion.1
  53.3 3.7 collective-permute-start
  60.4 4.5 collective-permute-done.1
  68.6 78.8 %all-gather.6.cloned.1.call-done = bf16[128,4,120,120]{3,2,1,0:T(8,128)(2,1)} async-done(((bf16[2,4,120,120]{3,2,1,0:T(8,128)(2,1)}), bf16[128,4,120,120]{3,2,1,0:T(8,128)(2,1)}) %all-gather.6.cloned.1.call-update) | async-done | bytes 14745616 | tf_op jit(solution)/shard_map/all_gather | solution.py:120
  147.4 222.5 %while.16 = (s32[]{:T(128)}, f32[4,64,4,120]{3,1,0,2:T(8,128)}, bf16[128,4,120,120]{3,2,1,0:T(8,128)(2,1)}, bf16[4,192,4,120]{3,1,0,2:T(8,128)(2,1)S(1)}, s32[]{...) while((s32[]{:T(128)}, f32[4,64,4,120]{3,1,0,2:T(8,128)}, ...), condition=%wide.region_5.6_spmd.clone, body=%wide.region_4.5_spmd.clone.sunk | while | flops 472105024 | bytes 34530440 | solution.py:75
  147.4 2.9 constant_dynamic-slice_fusion.20
  150.4 7.1 %concatenate.26 = bf16[4,64,4,1920]{3,1,0,2:T(8,128)(2,1)} concatenate(bf16[4,64,4,120]{3,1,0,2:T(8,128)(2,1)} %get-tuple-element.236, bf16[4,64,4,120]{3,1,0,2:T(8,128)(2,1)} %get-tuple-element.237, bf16[4,64,4,120]{3,1,0,2:T(8,128)(2,1)} %get-tuple-element.238, bf16[4,64,4,120]{3,1,0,2:T(8,128)(2,1)} %get-tuple-element.239, bf16[4,64,4,120]{3,1,0,2:T(8,128)(2,1)} %get-tuple-element.240, ...), dimensions={3} | concatenate | bytes 7864320 | tf_op jit(solution)/shard_map/while/body/eval_jaxpr/concatenate | solution.py:68
  157.5 3.0 constant_dynamic-slice_fusion.19
  160.6 4.4 copy.47
  165.0 4.6 reshape.314
  169.6 3.8 fusion.187
  174.3 3.0 constant_dynamic-slice_fusion.20
  177.3 7.1 %concatenate.26 = bf16[4,64,4,1920]{3,1,0,2:T(8,128)(2,1)} concatenate(bf16[4,64,4,120]{3,1,0,2:T(8,128)(2,1)} %get-tuple-element.236, bf16[4,64,4,120]{3,1,0,2:T(8,128)(2,1)} %get-tuple-element.237, bf16[4,64,4,120]{3,1,0,2:T(8,128)(2,1)} %get-tuple-element.238, bf16[4,64,4,120]{3,1,0,2:T(8,128)(2,1)} %get-tuple-element.239, bf16[4,64,4,120]{3,1,0,2:T(8,128)(2,1)} %get-tuple-element.240, ...), dimensions={3} | concatenate | bytes 7864320 | tf_op jit(solution)/shard_map/while/body/eval_jaxpr/concatenate | solution.py:68
  184.5 3.0 constant_dynamic-slice_fusion.19
  187.5 4.4 copy.47
  191.9 4.6 reshape.314
  196.5 3.8 fusion.187
  200.3 1.9 select_add_fusion.2
  202.3 3.0 constant_dynamic-slice_fusion.20
  205.2 7.1 %concatenate.26 = bf16[4,64,4,1920]{3,1,0,2:T(8,128)(2,1)} concatenate(bf16[4,64,4,120]{3,1,0,2:T(8,128)(2,1)} %get-tuple-element.236, bf16[4,64,4,120]{3,1,0,2:T(8,128)(2,1)} %get-tuple-element.237, bf16[4,64,4,120]{3,1,0,2:T(8,128)(2,1)} %get-tuple-element.238, bf16[4,64,4,120]{3,1,0,2:T(8,128)(2,1)} %get-tuple-element.239, bf16[4,64,4,120]{3,1,0,2:T(8,128)(2,1)} %get-tuple-element.240, ...), dimensions={3} | concatenate | bytes 7864320 | tf_op jit(solution)/shard_map/while/body/eval_jaxpr/concatenate | solution.py:68
  212.4 3.0 constant_dynamic-slice_fusion.19
  215.4 4.4 copy.47
  219.9 4.6 reshape.314
  224.4 3.8 fusion.187
  230.2 3.0 constant_dynamic-slice_fusion.20
  233.2 7.1 %concatenate.26 = bf16[4,64,4,1920]{3,1,0,2:T(8,128)(2,1)} concatenate(bf16[4,64,4,120]{3,1,0,2:T(8,128)(2,1)} %get-tuple-element.236, bf16[4,64,4,120]{3,1,0,2:T(8,128)(2,1)} %get-tuple-element.237, bf16[4,64,4,120]{3,1,0,2:T(8,128)(2,1)} %get-tuple-element.238, bf16[4,64,4,120]{3,1,0,2:T(8,128)(2,1)} %get-tuple-element.239, bf16[4,64,4,120]{3,1,0,2:T(8,128)(2,1)} %get-tuple-element.240, ...), dimensions={3} | concatenate | bytes 7864320 | tf_op jit(solution)/shard_map/while/body/eval_jaxpr/concatenate | solution.py:68
  240.4 3.0 constant_dynamic-slice_fusion.19
  243.4 4.4 copy.47
  247.8 4.6 reshape.314
  252.4 3.8 fusion.187
  258.2 2.9 constant_dynamic-slice_fusion.20
  261.1 7.1 %concatenate.26 = bf16[4,64,4,1920]{3,1,0,2:T(8,128)(2,1)} concatenate(bf16[4,64,4,120]{3,1,0,2:T(8,128)(2,1)} %get-tuple-element.236, bf16[4,64,4,120]{3,1,0,2:T(8,128)(2,1)} %get-tuple-element.237, bf16[4,64,4,120]{3,1,0,2:T(8,128)(2,1)} %get-tuple-element.238, bf16[4,64,4,120]{3,1,0,2:T(8,128)(2,1)} %get-tuple-element.239, bf16[4,64,4,120]{3,1,0,2:T(8,128)(2,1)} %get-tuple-element.240, ...), dimensions={3} | concatenate | bytes 7864320 | tf_op jit(solution)/shard_map/while/body/eval_jaxpr/concatenate | solution.py:68
  268.3 3.0 constant_dynamic-slice_fusion.19
  271.3 4.4 copy.47
  275.7 4.6 reshape.314
  280.3 3.8 fusion.187
  286.1 3.0 constant_dynamic-slice_fusion.20
  289.1 7.1 %concatenate.26 = bf16[4,64,4,1920]{3,1,0,2:T(8,128)(2,1)} concatenate(bf16[4,64,4,120]{3,1,0,2:T(8,128)(2,1)} %get-tuple-element.236, bf16[4,64,4,120]{3,1,0,2:T(8,128)(2,1)} %get-tuple-element.237, bf16[4,64,4,120]{3,1,0,2:T(8,128)(2,1)} %get-tuple-element.238, bf16[4,64,4,120]{3,1,0,2:T(8,128)(2,1)} %get-tuple-element.239, bf16[4,64,4,120]{3,1,0,2:T(8,128)(2,1)} %get-tuple-element.240, ...), dimensions={3} | concatenate | bytes 7864320 | tf_op jit(solution)/shard_map/while/body/eval_jaxpr/concatenate | solution.py:68
  296.2 3.0 constant_dynamic-slice_fusion.19
  299.2 4.4 copy.47
  303.7 4.6 reshape.314
  308.3 3.8 fusion.187
  314.0 3.0 constant_dynamic-slice_fusion.20
  317.0 7.1 %concatenate.26 = bf16[4,64,4,1920]{3,1,0,2:T(8,128)(2,1)} concatenate(bf16[4,64,4,120]{3,1,0,2:T(8,128)(2,1)} %get-tuple-element.236, bf16[4,64,4,120]{3,1,0,2:T(8,128)(2,1)} %get-tuple-element.237, bf16[4,64,4,120]{3,1,0,2:T(8,128)(2,1)} %get-tuple-element.238, bf16[4,64,4,120]{3,1,0,2:T(8,128)(2,1)} %get-tuple-element.239, bf16[4,64,4,120]{3,1,0,2:T(8,128)(2,1)} %get-tuple-element.240, ...), dimensions={3} | concatenate | bytes 7864320 | tf_op jit(solution)/shard_map/while/body/eval_jaxpr/concatenate | solution.py:68
  324.2 3.0 constant_dynamic-slice_fusion.19
  327.2 4.4 copy.47
  331.6 4.6 reshape.314
  336.2 3.8 fusion.187
  342.0 3.0 constant_dynamic-slice_fusion.20
  345.0 7.1 %concatenate.26 = bf16[4,64,4,1920]{3,1,0,2:T(8,128)(2,1)} concatenate(bf16[4,64,4,120]{3,1,0,2:T(8,128)(2,1)} %get-tuple-element.236, bf16[4,64,4,120]{3,1,0,2:T(8,128)(2,1)} %get-tuple-element.237, bf16[4,64,4,120]{3,1,0,2:T(8,128)(2,1)} %get-tuple-element.238, bf16[4,64,4,120]{3,1,0,2:T(8,128)(2,1)} %get-tuple-element.239, bf16[4,64,4,120]{3,1,0,2:T(8,128)(2,1)} %get-tuple-element.240, ...), dimensions={3} | concatenate | bytes 7864320 | tf_op jit(solution)/shard_map/while/body/eval_jaxpr/concatenate | solution.py:68
  352.1 3.0 constant_dynamic-slice_fusion.19
  355.2 4.4 copy.47
  359.6 4.6 reshape.314
  364.2 3.8 fusion.187
  373.2 3.8 fusion.4
  379.6 18.8 %reduce-scatter.2.cloned.1.call-done = f32[1,64,1024]{2,1,0:T(8,128)} async-done(((f32[4,64,1024]{2,1,0:T(8,128)}), f32[1,64,1024]{2,1,0:T(8,128)}) %reduce-scatter.2.cloned.1.call-update) | async-done | bytes 262160 | tf_op jit(solution)/shard_map/reduce_scatter | solution.py:127
  398.5 2.3 fusion.34
  401.2 41.0 %all-gather.10.cloned.1.call-done = bf16[1024,1024]{1,0:T(8,128)(2,1)} async-done(((bf16[64,1024]{1,0:T(8,128)(2,1)}), bf16[1024,1024]{1,0:T(8,128)(2,1)}) %all-gather.10.cloned.1.call-update) | async-done | bytes 2097168 | tf_op jit(solution)/shard_map/all_gather | solution.py:134
  442.2 2.3 convolution_bitcast_fusion
  444.6 48.5 %gather_fusion = f32[6400]{0:T(1024)S(1)} fusion(f32[1,64,1024]{2,1,0:T(8,128)S(1)} %convolution_bitcast_fusion, s32[6400]{0:T(1024)S(1)} %reshape.273), kind=kCustom, calls=%fused_computation | custom fusion | bytes 128000 | tf_op jit(solution)/shard_map/vmap(jit(take_along_axis))/gather | solution.py:47
  493.2 2.1 fusion
  495.3 35.1 %gather_fusion.1 = f32[6400]{0:T(1024)S(1)} fusion(f32[1,1024]{1,0:T(1,128)S(1)} %bitcast.84, s32[6400]{0:T(1024)S(1)} %reshape.281), kind=kCustom, calls=%fused_computation.1 | custom fusion | bytes 102400 | tf_op jit(solution)/shard_map/vmap()/gather | solution.py:48
  (67 shorter events, 33.9 us)
Async XLA Ops:
  6.5 391.9 %copy-start = (bf16[1024,1024]{1,0:T(8,128)(2,1)S(1)}, bf16[1024,1024]{1,0:T(8,128)(2,1)}, u32[]{:S(2)}) copy-start(bf16[1024,1024]{1,0:T(8,128)(2,1)} %param.20) | copy-start | bytes 6291460
  6.5 40.5 %all-gather.8.cloned.1.call-start = ((), (), s32[]{:S(2)}) async-start(), calls=%async_computation.3 | async-start | bytes 2621440 | tf_op jit(solution)/shard_map/all_gather | solution.py:99
  7.6 43.2 %copy-start.6 = (bf16[480]{0:T(512)(128)(2,1)S(1)}, bf16[480]{0:T(512)(128)(2,1)}, u32[]{:S(2)}) copy-start(bf16[480]{0:T(512)(128)(2,1)} %param.16) | copy-start | bytes 2884
  9.7 137.8 %all-gather.6.cloned.1.call-start = ((), (), s32[]{:S(2)}) async-start(), calls=%async_computation.1 | async-start | bytes 15974400 | tf_op jit(solution)/shard_map/all_gather | solution.py:120
  10.4 388.0 %reduce-scatter.2.cloned.1.call-start = ((), (), s32[]{:S(2)}) async-start(), calls=%async_computation.2 | async-start | bytes 1310720 | tf_op jit(solution)/shard_map/reduce_scatter | solution.py:127
  53.3 94.1 %copy-start.2 = (bf16[4,64,480]{2,1,0:T(8,128)(2,1)}, bf16[4,64,480]{2,1,0:T(8,128)(2,1)S(1)}, u32[]{:S(2)}) copy-start(bf16[4,64,480]{2,1,0:T(8,128)(2,1)S(1)} %fusion.1) | copy-start | bytes 737284
  53.3 7.0 %collective-permute-start = (bf16[4,64,480]{2,1,0:T(8,128)(2,1)S(1)}, bf16[4,64,480]{2,1,0:T(8,128)(2,1)S(1)}, u32[]{:S(2)}, u32[]{:S(2)}) collective-permute-start(bf16[4,64,480]{2,1,0:T(8,128)(2,1)S(1)} %fusion.1), channel_id=1, source_target_pairs={{0,4},{4,8},{8,12},{12,16},{16,20},{20,24},{24,28},{28,32},{32,36}... | collective-permute-start | bytes 737288 | tf_op jit(solution)/shard_map/ppermute | solution.py:18
  57.1 7.8 %collective-permute-start.1 = (bf16[4,64,480]{2,1,0:T(8,128)(2,1)S(1)}, bf16[4,64,480]{2,1,0:T(8,128)(2,1)}, u32[]{:S(2)}, u32[]{:S(2)}) collective-permute-start(bf16[4,64,480]{2,1,0:T(8,128)(2,1)S(1)} %fusion.1), channel_id=1, source_target_pairs={{4,0},{8,4},{12,8},{16,12},{20,16},{24,20},{28,24},{32,28},{36,32}... | collective-permute-start | bytes 737288 | tf_op jit(solution)/shard_map/ppermute | solution.py:21
  369.9 3.2 copy-start.3
  373.2 4.1 copy-start.5
  377.0 23.9 %copy-start.4 = (s32[1,64,100]{2,1,0:T(8,128)S(1)}, s32[1,64,100]{2,1,0:T(8,128)}, u32[]{:S(2)}) copy-start(s32[1,64,100]{2,1,0:T(8,128)} %param.23) | copy-start | bytes 76804
  377.0 65.3 %all-gather.10.cloned.1.call-start = ((), (), s32[]{:S(2)}) async-start(), calls=%async_computation.4 | async-start | bytes 2228224 | tf_op jit(solution)/shard_map/all_gather | solution.py:134
  398.5 43.8 %copy-start.1 = (f32[1,64,1024]{2,1,0:T(8,128)S(1)}, f32[1,64,1024]{2,1,0:T(8,128)}, u32[]{:S(2)}) copy-start(f32[1,64,1024]{2,1,0:T(8,128)} %reduce-scatter.2.cloned.1.call-done) | copy-start | bytes 786436
Sparse Core Ops, SparseCore 0:
  9.8 37.2 all-gather.7
  49.8 97.5 all-gather.5
  377.1 21.3 reduce-scatter.1
  400.9 41.2 all-gather.9
